TPU v7x, 32 devices: a whole 2x2x4 slice. The times are simulated.
32 devices in a mesh: mem: 8 (over z, x), fsdp: 4 (over y, core).
Axes of the slice: x: 2, y: 2, z: 4, core: 2. Of those that a mesh axis runs over, the one named last changes fastest.
Arguments:
- layer_input: bfloat16 [4096, 4096], P(('mem', 'fsdp')), may hold values from -6 to 6
- w_query: bfloat16 [4096, 2048], P('mem', 'fsdp'), may hold values from -0.09375 to 0.09375
- local_kv: bfloat16 [2, 4096, 2048], P(None, 'mem', 'fsdp'), may hold values from -200 to 200, as said below
- memory_kv: bfloat16 [128, 2, 128, 2048], P('mem', None, None, 'fsdp'), may hold values from -200 to 200
- memory_ids: int32 [32, 4], P('mem'), may hold values from 0 to 127, as said below
- grad_out: bfloat16 [4096, 2048], P('mem', 'fsdp'), may hold values from -6 to 6
Outputs:
- attended: bfloat16 [4096, 2048], P('mem', 'fsdp')
- grad_input: bfloat16 [4096, 4096], P(('mem', 'fsdp'))
Inputs may be any that keep to these rules, and one draw needn't show every extreme that they name: `memory_ids`: within the tiles of one local context (4 tiles), all named blocks of one owner (same id // 16) are one and the same block, and every owner is named by some tile of every local context; each tile names 4 blocks of different owners. `local_kv`: keys and values of the document's tokens.
All inputs are finite; a program needn't handle non-finite values.
Results may differ from a plain program's by a relative error of at most 0.025.
The roundings to bfloat16 on the way count: a program that leaves them out, or rounds other values in their place, can miss the bound.
Values may be sent and summed in bfloat16 or wider, within the bound.
A program may use at most 128 MiB of HBM per device.

v0:
```python
import math

import jax
import jax.numpy as jnp
from jax import lax
from jax.sharding import PartitionSpec as P

HD = 128
BLK = 128
TOPK = 4
MB_DEV = 16


NEG_FILL = -1e30


def attend_context(queries, context_kv, tile_kv, grad_rows):
    ctx_len, width = queries.shape
    heads_count = width // HD
    tiles_count = tile_kv.shape[0]
    mem_keys_count = TOPK * BLK
    score_scale = 1.0 / math.sqrt(HD)
    query_heads = queries.reshape(ctx_len, heads_count, HD)
    query_tiles = query_heads.reshape(tiles_count, BLK, heads_count, HD)
    local_keys = context_kv[0].reshape(ctx_len, heads_count, HD)
    local_values = context_kv[1].reshape(ctx_len, heads_count, HD)
    mem_keys = tile_kv[:, :, 0].reshape(tiles_count, mem_keys_count, heads_count, HD)
    mem_values = tile_kv[:, :, 1].reshape(tiles_count, mem_keys_count, heads_count, HD)
    grad_heads = grad_rows.reshape(ctx_len, heads_count, HD)
    grad_tiles = grad_heads.reshape(tiles_count, BLK, heads_count, HD)
    mem_scores = (
        jnp.einsum("tqhd,tkhd->htqk", query_tiles, mem_keys, preferred_element_type=jnp.float32)
        * score_scale
    )
    mem_scores = mem_scores.reshape(heads_count, ctx_len, mem_keys_count)
    loc_scores = (
        jnp.einsum("qhd,khd->hqk", query_heads, local_keys, preferred_element_type=jnp.float32)
        * score_scale
    )
    positions = jnp.arange(ctx_len, dtype=jnp.int32)
    causal = positions[:, None] >= positions[None, :]
    loc_scores = jnp.where(causal[None], loc_scores, NEG_FILL)
    row_max = jnp.maximum(jnp.max(mem_scores, axis=2), jnp.max(loc_scores, axis=2))
    mem_exp = jnp.exp(mem_scores - row_max[:, :, None])
    loc_exp = jnp.exp(loc_scores - row_max[:, :, None])
    total = jnp.sum(mem_exp, axis=2) + jnp.sum(loc_exp, axis=2)
    mem_prob = mem_exp / total[:, :, None]
    loc_prob = loc_exp / total[:, :, None]
    mem_weights = mem_prob.astype(jnp.bfloat16).reshape(
        heads_count, tiles_count, BLK, mem_keys_count
    )
    loc_weights = loc_prob.astype(jnp.bfloat16)
    mem_part = jnp.einsum(
        "htqk,tkhd->tqhd", mem_weights, mem_values, preferred_element_type=jnp.float32
    )
    loc_part = jnp.einsum(
        "hqk,khd->qhd", loc_weights, local_values, preferred_element_type=jnp.float32
    )
    attended = (
        (mem_part.reshape(ctx_len, heads_count, HD) + loc_part)
        .reshape(ctx_len, width)
        .astype(jnp.bfloat16)
    )
    mem_dprob = jnp.einsum(
        "tqhd,tkhd->htqk", grad_tiles, mem_values, preferred_element_type=jnp.float32
    )
    mem_dprob = mem_dprob.reshape(heads_count, ctx_len, mem_keys_count)
    loc_dprob = jnp.einsum(
        "qhd,khd->hqk", grad_heads, local_values, preferred_element_type=jnp.float32
    )
    delta = jnp.sum(mem_prob * mem_dprob, axis=2) + jnp.sum(loc_prob * loc_dprob, axis=2)
    mem_dscore = (mem_prob * (mem_dprob - delta[:, :, None])).astype(jnp.bfloat16)
    loc_dscore = (loc_prob * (loc_dprob - delta[:, :, None])).astype(jnp.bfloat16)
    mem_dscore = mem_dscore.reshape(heads_count, tiles_count, BLK, mem_keys_count)
    mem_grad = jnp.einsum(
        "htqk,tkhd->tqhd", mem_dscore, mem_keys, preferred_element_type=jnp.float32
    )
    loc_grad = jnp.einsum(
        "hqk,khd->qhd", loc_dscore, local_keys, preferred_element_type=jnp.float32
    )
    grad_queries = ((mem_grad.reshape(ctx_len, heads_count, HD) + loc_grad) * score_scale).reshape(
        ctx_len, width
    )
    return (attended, grad_queries.astype(jnp.bfloat16))


def local(layer_input, w_query, local_kv, memory_kv, memory_ids, grad_out):
    owners_count = lax.axis_size("mem")
    owner_of = memory_ids // MB_DEV
    owner_range = jnp.arange(owners_count, dtype=jnp.int32)
    matches = owner_of[:, :, None] == owner_range[None, None, :]
    local_index = (memory_ids % MB_DEV)[:, :, None]
    wanted_local = jnp.max(jnp.where(matches, local_index, 0), axis=(0, 1)).reshape(owners_count, 1)
    asked = lax.all_to_all(wanted_local, "mem", split_axis=0, concat_axis=0, tiled=True)
    outgoing = jnp.take(memory_kv, asked[:, 0], axis=0)
    received = lax.all_to_all(outgoing, "mem", split_axis=0, concat_axis=0, tiled=True)
    tile_kv = jnp.take(received, owner_of, axis=0)
    weight_slice = lax.all_gather(w_query, "mem", axis=0, tiled=True)
    queries = jnp.dot(
        lax.all_gather(layer_input, "fsdp", axis=0, tiled=True),
        weight_slice,
        preferred_element_type=jnp.float32,
    ).astype(jnp.bfloat16)
    attended, grad_queries = attend_context(queries, local_kv, tile_kv, grad_out)
    grad_input = lax.psum_scatter(
        lax.dot_general(
            grad_queries, weight_slice, (((1,), (1,)), ((), ())), preferred_element_type=jnp.float32
        ).astype(jnp.bfloat16),
        "fsdp",
        scatter_dimension=0,
        tiled=True,
    )
    return (attended, grad_input)


def solution(mesh):
    placed = (
        P(("mem", "fsdp"), None),
        P("mem", "fsdp"),
        P(None, "mem", "fsdp"),
        P("mem", None, None, "fsdp"),
        P("mem", None),
        P("mem", "fsdp"),
    )
    return jax.shard_map(
        local,
        mesh=mesh,
        in_specs=placed,
        out_specs=(P("mem", "fsdp"), P(("mem", "fsdp"), None)),
        check_vma=False,
    )
```

profile of v0, /device:TPU:0, one launch (start us, length us, event | category | flops | bytes accessed | tf_op | source)
XLA Modules:
  0.0 231.0 jit_solution(12584059387113015631)
XLA Ops:
  7.9 0.7 all-gather.5.cloned.1.call-update
  10.2 13.6 %all_to_all.20 = s32[8,1,1]{2,1,0:T(1,128)S(1)} all-to-all(s32[8,1,1]{2,1,0:T(1,128)S(1)} %copy.94), channel_id=1, replica_groups=mesh['mem'=8,'fsdp'=4] {'mem'}, dimensions={0} | all-to-all | bytes 64 | tf_op jit(solution)/shard_map/all_to_all | solution.py:94
  24.0 2.9 %gather_fusion = bf16[8,2,128,512]{3,2,1,0:T(8,128)(2,1)S(1)} fusion(bf16[16,2,128,512]{3,2,1,0:T(8,128)(2,1)} %param.9, s32[1024]{0:T(1024)S(1)} %pad_clamp_fusion.1), kind=kCustom, calls=%fused_computation | custom fusion | bytes 4194336 | tf_op jit(solution)/shard_map/jit(_take)/gather | solution.py:95
  26.9 1.7 broadcast_select_fusion
  28.6 3.6 %all-to-all-start.1 = ((bf16[8,2,128,512]{3,2,1,0:T(8,128)(2,1)}), bf16[8,2,128,512]{3,2,1,0:T(8,128)(2,1)S(1)}, u32[]{:S(2)}, u32[]{:S(2)}) async-start(bf16[8,2,128,512]{3,2,1,0:T(8,128)(2,1)} %broadcast_select_fusion), calls=%async_computation.1 | async-start | bytes 4194304 | tf_op jit(solution)/shard_map/all_to_all | solution.py:96
  32.3 0.9 reshape_reshape.7
  33.3 1.3 fusion.56
  34.6 1.0 copy.104
  35.9 60.2 %all-to-all-done.1 = bf16[8,2,128,512]{3,2,1,0:T(8,128)(2,1)S(1)} async-done(((bf16[8,2,128,512]{3,2,1,0:T(8,128)(2,1)}), bf16[8,2,128,512]{3,2,1,0:T(8,128)(2,1)S(1)}, u32[]{:S(2)}, u32[]{:S(2)}) %all-to-all-start.1) | async-done | bytes 2097184 | tf_op jit(solution)/shard_map/all_to_all | solution.py:96
  96.1 2.8 %gather_fusion.1 = bf16[16,2,128,512]{3,2,1,0:T(8,128)(2,1)} fusion(bf16[8,2,128,512]{3,2,1,0:T(8,128)(2,1)S(1)} %all-to-all-done.1, s32[1024]{0:T(1024)S(1)} %pad_clamp_fusion), kind=kCustom, calls=%fused_computation.1 | custom fusion | bytes 8388672 | tf_op jit(solution)/shard_map/jit(_take)/gather | solution.py:97
  98.8 2.6 %copy_select_fusion = bf16[4,4,2,128,512]{4,3,1,0,2:T(8,128)(2,1)S(1)} fusion(bf16[4,4,2,128,512]{4,3,2,1,0:T(8,128)(2,1)} %bitcast.77, pred[4,4]{1,0:T(4,128)(4,1)S(1)} %get-tuple-element.12), kind=kLoop, calls=%fused_computation.8 | loop fusion | flops 2097152 | bytes 8388624 | tf_op jit(solution)/shard_map/jit(_take)/select_n | solution.py:97
  101.5 2.5 %fusion.55 = (bf16[4,4,1,128,512]{4,3,1,0,2:T(8,128)(2,1)}, bf16[4,4,1,128,512]{4,3,1,0,2:T(8,128)(2,1)}) fusion(bf16[4,4,2,128,512]{4,3,1,0,2:T(8,128)(2,1)S(1)} %copy_select_fusion), kind=kLoop, calls=%fused_computation.73 | loop fusion | bytes 8388608 | tf_op jit(solution)/shard_map/slice | solution.py:27
  104.0 2.6 %reshape_squeeze.13 = bf16[4,512,4,128]{3,2,1,0:T(4,128)(2,1)S(1)} reshape(bf16[4,4,1,128,512]{4,3,1,0,2:T(8,128)(2,1)} %get-tuple-element.16) | data formatting | bytes 4194304 | tf_op jit(solution)/shard_map/reshape;squeeze | solution.py:27
  106.6 4.0 %reshape_squeeze.12 = bf16[4,512,4,128]{3,2,1,0:T(4,128)(2,1)} reshape(bf16[4,4,1,128,512]{4,3,1,0,2:T(8,128)(2,1)} %get-tuple-element.17) | data formatting | bytes 4194304 | tf_op jit(solution)/shard_map/reshape;squeeze | solution.py:28
  110.6 26.8 %all-gather.5.cloned.1.call-done = bf16[4096,512]{1,0:T(8,128)(2,1)} async-done(((bf16[512,512]{1,0:T(8,128)(2,1)}), bf16[4096,512]{1,0:T(8,128)(2,1)}) %all-gather.5.cloned.1.call-update) | async-done | bytes 4194320 | tf_op jit(solution)/shard_map/all_gather | solution.py:98
  137.4 6.6 %convolution_convert_fusion.1 = bf16[512,512]{0,1:T(8,128)(2,1)} fusion(bf16[512,4096]{1,0:T(8,128)(2,1)} %all-gather.3.cloned.1.call-done, bf16[4096,512]{1,0:T(8,128)(2,1)} %all-gather.5.cloned.1.call-done), kind=kOutput, calls=%fused_computation.43 | convolution fusion | flops 2147745792 | bytes 8912896 | tf_op jit(solution)/shard_map/dot_general | solution.py:99
  144.0 2.0 reshape_reshape.6
  146.0 4.0 %fusion.3 = (f32[4,512]{1,0:T(4,128)S(1)}, f32[4,512,512]{1,2,0:T(8,128)}) fusion(pred[512,512]{0,1:T(8,128)(4,1)S(1)} %iota_compare_fusion, bf16[512,4,128]{0,2,1:T(8,128)(2,1)} %bitcast.82, bf16[512,4,128]{0,2,1:T(8,128)(2,1)S(1)} %bitcast.80), kind=kOutput, calls=%fused_computation.15 | convolution fusion | flops 271579136 | bytes 5513216 | tf_op jit(solution)/shard_map/qhd,khd->hqk/dot_general | solution.py:37
  149.9 4.0 %multiply_reduce_fusion.1 = (f32[4,4,128]{2,1,0:T(4,128)S(1)}, f32[4,4,128,512]{3,2,1,0:T(8,128)}) fusion(bf16[4,512,4,128]{3,2,1,0:T(4,128)(2,1)S(1)} %reshape_squeeze.13, bf16[4,128,4,128]{1,0,3,2:T(4,128)(2,1)} %reshape_reshape.6), kind=kOutput, calls=%fused_computation.14 | convolution fusion | flops 270530560 | bytes 6823936 | tf_op jit(solution)/shard_map/tqhd,tkhd->htqk/dot_general | solution.py:32
  153.9 0.9 fusion.7
  154.9 3.4 %fusion.5 = f32[4,4,128]{2,1,0:T(4,128)S(1)} fusion(f32[4,4,128,512]{3,2,1,0:T(8,128)} %get-tuple-element.21, f32[4,4,128]{2,1,0:T(4,128)S(1)} %max.10), kind=kLoop, calls=%fused_computation.17 | loop fusion | flops 3143680 | bytes 4210688 | tf_op jit(solution)/shard_map/reduce_sum | solution.py:46
  158.3 4.8 %multiply_reduce_fusion = (f32[4,512]{1,0:T(4,128)S(1)}, f32[4,512,512]{1,2,0:T(8,128)}) fusion(f32[4,512]{1,0:T(4,128)S(1)} %bitcast_add_fusion.1, f32[4,512]{1,0:T(4,128)S(1)} %bitcast_maximum_fusion, f32[4,512,512]{1,2,0:T(8,128)S(1)} %copy-done.2, pred[512,512]{0,1:T(8,128)(4,1)S(1)} %iota_compare_fusion, bf16[512,4,128]{0,2,1:T(8,128)(2,1)} %bitcast.83, ...), kind=kOutput, calls=%fused_computation.10 | convolution fusion | flops 274724864 | bytes 9723904 | tf_op jit(solution)/shard_map/qhd,khd->hqk/dot_general | solution.py:68
  163.1 4.9 %fusion = (f32[4,4,128]{2,1,0:T(4,128)S(1)}, f32[4,4,512,128]{2,3,1,0:T(8,128)S(1)}) fusion(f32[4,4,128]{2,1,0:T(4,128)S(1)} %add.58, f32[4,4,128]{2,1,0:T(4,128)S(1)} %max.10, f32[4,4,128,512]{3,2,1,0:T(8,128)} %get-tuple-element.21, bf16[4,128,4,128]{3,2,1,0:T(4,128)(2,1)} %reshape_reshape.7, bf16[4,512,4,128]{3,2,1,0:T(4,128)(2,1)} %reshape_squeeze.12), kind=kOutput, calls=%fused_computation.5 | convolution fusion | flops 273676288 | bytes 11034624 | tf_op jit(solution)/shard_map/tqhd,tkhd->htqk/dot_general | solution.py:64
  168.1 2.3 %fusion.2 = (bf16[4,4,128,512]{3,2,1,0:T(8,128)(2,1)S(1)}, bf16[4,4,128,512]{3,2,1,0:T(8,128)(2,1)}) fusion(f32[4,4,512,128]{2,3,1,0:T(8,128)S(1)} %get-tuple-element.25, f32[4,4,128]{2,1,0:T(4,128)S(1)} %add.61, f32[4,4,128]{2,1,0:T(4,128)S(1)} %add.58, f32[4,4,128]{2,1,0:T(4,128)S(1)} %max.10, f32[4,4,128,512]{3,2,1,0:T(8,128)S(1)} %copy-done), kind=kLoop, calls=%fused_computation.7 | loop fusion | flops 7340032 | bytes 12607488 | tf_op jit(solution)/shard_map/convert_element_type | solution.py:72
  170.4 0.7 fusion.33
  171.6 5.3 %fusion.41 = bf16[512,4,128]{0,2,1:T(8,128)(2,1)S(1)} fusion(f32[512,4,128]{0,2,1:T(8,128)S(1)} %copy.116, bf16[512,4,128]{0,2,1:T(8,128)(2,1)S(1)} %bitcast.81, f32[4,512,512]{1,2,0:T(8,128)} %get-tuple-element.27, f32[4,512]{1,0:T(4,128)S(1)} %bitcast_add_fusion, f32[4,512,512]{1,2,0:T(8,128)} %get-tuple-element.23, f32[4,512]{1,0:T(4,128)S(1)} %bitcast_add_fusion.1, ...), kind=kOutput, calls=%fused_computation.42 | convolution fusion | flops 276561920 | bytes 10772480 | tf_op jit(solution)/shard_map/hqk,khd->qhd/dot_general | solution.py:78
  176.9 4.3 %convolution_convert_fusion = bf16[512,4096]{1,0:T(8,128)(2,1)} fusion(bf16[512,512]{0,1:T(8,128)(2,1)S(1)} %bitcast.90, bf16[4096,512]{1,0:T(8,128)(2,1)S(1)} %copy-done.6), kind=kOutput, calls=%fused_computation.2 | convolution fusion | flops 2149580800 | bytes 8912896 | tf_op jit(solution)/shard_map/dot_general | solution.py:106
  181.2 1.6 copy-done.3
  182.8 2.4 %fusion.28 = f32[4,128,4,128]{3,1,2,0:T(8,128)S(1)} fusion(bf16[4,512,4,128]{3,2,1,0:T(4,128)(2,1)S(1)} %copy-done.3, bf16[4,4,128,512]{3,2,1,0:T(8,128)(2,1)} %get-tuple-element.15), kind=kOutput, calls=%fused_computation.37 | convolution fusion | flops 268435456 | bytes 5242880 | tf_op jit(solution)/shard_map/htqk,tkhd->tqhd/dot_general | solution.py:53
  185.6 3.7 %fusion.42 = bf16[512,4,128]{0,2,1:T(8,128)(2,1)S(1)} fusion(f32[512,4,128]{0,2,1:T(8,128)S(1)} %copy.106, bf16[512,4,128]{0,2,1:T(8,128)(2,1)S(1)} %bitcast.84, f32[4,512,512]{1,2,0:T(8,128)} %get-tuple-element.23, f32[4,512]{1,0:T(4,128)S(1)} %bitcast_add_fusion.1, f32[4,512]{1,0:T(4,128)S(1)} %bitcast_maximum_fusion, ...), kind=kOutput, calls=%fused_computation.44 | convolution fusion | flops 274202624 | bytes 6569984 | tf_op jit(solution)/shard_map/hqk,khd->qhd/dot_general | solution.py:56
  189.3 1.0 copy.117
  190.3 34.2 %reduce-scatter.2.cloned.1.call-done = bf16[128,4096]{1,0:T(8,128)(2,1)} async-done(((bf16[512,4096]{1,0:T(8,128)(2,1)}), bf16[128,4096]{1,0:T(8,128)(2,1)}) %reduce-scatter.2.cloned.1.call-update) | async-done | bytes 1048592 | tf_op jit(solution)/shard_map/reduce_scatter | solution.py:105
  (45 shorter events, 4.0 us)
Async XLA Ops:
  7.2 103.4 %all-gather.3.cloned.1.call-start = ((), (), s32[]{:S(2)}) async-start(), calls=%async_computation.3 | async-start | bytes 5242880 | tf_op jit(solution)/shard_map/all_gather | solution.py:100
  7.9 129.5 %all-gather.5.cloned.1.call-start = ((), (), s32[]{:S(2)}) async-start(), calls=%async_computation.4 | async-start | bytes 4718592 | tf_op jit(solution)/shard_map/all_gather | solution.py:98
  26.9 5.4 %copy-start.4 = (bf16[512,512]{1,0:T(8,128)(2,1)S(1)}, bf16[512,512]{1,0:T(8,128)(2,1)}, u32[]{:S(2)}) copy-start(bf16[512,512]{1,0:T(8,128)(2,1)} %param.11) | copy-start | bytes 1572868
  28.6 67.5 %all-to-all-start.1 = ((bf16[8,2,128,512]{3,2,1,0:T(8,128)(2,1)}), bf16[8,2,128,512]{3,2,1,0:T(8,128)(2,1)S(1)}, u32[]{:S(2)}, u32[]{:S(2)}) async-start(bf16[8,2,128,512]{3,2,1,0:T(8,128)(2,1)} %broadcast_select_fusion), calls=%async_computation.1 | async-start | bytes 4194304 | tf_op jit(solution)/shard_map/all_to_all | solution.py:96
  32.2 192.3 %reduce-scatter.2.cloned.1.call-start = ((), (), s32[]{:S(2)}) async-start(), calls=%async_computation.5 | async-start | bytes 5242880 | tf_op jit(solution)/shard_map/reduce_scatter | solution.py:105
  149.9 4.0 %copy-start.1 = (f32[4,512,512]{1,2,0:T(8,128)S(1)}, f32[4,512,512]{1,2,0:T(8,128)}, u32[]{:S(2)}) copy-start(f32[4,512,512]{1,2,0:T(8,128)} %get-tuple-element.23) | copy-start | bytes 12582916
  154.9 3.4 %copy-start.2 = (f32[4,512,512]{1,2,0:T(8,128)S(1)}, f32[4,512,512]{1,2,0:T(8,128)}, u32[]{:S(2)}) copy-start(f32[4,512,512]{1,2,0:T(8,128)} %get-tuple-element.23) | copy-start | bytes 12582916
  163.1 5.0 %copy-start = (f32[4,4,128,512]{3,2,1,0:T(8,128)S(1)}, f32[4,4,128,512]{3,2,1,0:T(8,128)}, u32[]{:S(2)}) copy-start(f32[4,4,128,512]{3,2,1,0:T(8,128)} %get-tuple-element.21) | copy-start | bytes 12582916
  171.6 5.3 %copy-start.6 = (bf16[4096,512]{1,0:T(8,128)(2,1)S(1)}, bf16[4096,512]{1,0:T(8,128)(2,1)}, u32[]{:S(2)}) copy-start(bf16[4096,512]{1,0:T(8,128)(2,1)} %all-gather.5.cloned.1.call-done) | copy-start | bytes 12582916
  181.2 1.6 copy-start.3
  182.8 2.8 %copy-start.5 = (bf16[1,512,512]{1,2,0:T(8,128)(2,1)S(1)}, bf16[1,512,512]{1,2,0:T(8,128)(2,1)}, u32[]{:S(2)}) copy-start(bf16[1,512,512]{1,2,0:T(8,128)(2,1)} %copy.104) | copy-start | bytes 1572868
Sparse Core Ops, SparseCore 0:
  9.5 37.1 all-gather.2
  48.9 88.4 all-gather.4
  181.4 43.1 reduce-scatter.1
where the time goes:
time: 232 us; the launch traced here: 231 us
  waiting for transfers between devices  123 us (53%)
  matrix products  40.6 us (18%)
  local copies, waits for them, and re-layouts  23.8 us (10%)
  between operations  14 us (6%)
  blocking collectives  13.6 us (6%)
  other arithmetic  12.8 us (6%)
  starting transfers between devices  3.72 us (2%)
    all_to_all x1, waiting for transfers between devices, local(): lax.all_to_all(outgoing, 'mem', split_axis=0, concat_axis=0, tiled=True)  60.2 us
    reduce_scatter x1, waiting for transfers between devices, local(): lax.psum_scatter(lax.dot_general(grad_queries, weight_slice, (((1,), (1,)...  34.2 us
    all_gather x1, waiting for transfers between devices, local(): weight_slice = lax.all_gather(w_query, 'mem', axis=0, tiled=True)  26.8 us
    all_to_all x1, blocking collectives, local(): lax.all_to_all(wanted_local, 'mem', split_axis=0, concat_axis=0, tiled=True)  13.6 us
    dot_general x1, matrix products, local(): jnp.dot(lax.all_gather(layer_input, 'fsdp', axis=0, tiled=True), weight_s...  6.63 us
    dot_general x1, matrix products, attend_context(): jnp.einsum('hqk,khd->qhd', loc_dscore, local_keys, preferred_element_type...  5.3 us
    dot_general x1, matrix products, attend_context(): jnp.einsum('tqhd,tkhd->htqk', grad_tiles, mem_values, preferred_element_t...  4.95 us
    dot_general x1, matrix products, attend_context(): jnp.einsum('qhd,khd->hqk', grad_heads, local_values, preferred_element_ty...  4.76 us
  transfers between devices with their start and end apart: 4, of which 3 were waited for; matrix products, arithmetic and copies ran while one was open for 14% of the time, Pallas kernels for 0%

commit v1 on v0

v1 whole, which is shorter than its diff:
```python
import functools
import math

import jax
import jax.numpy as jnp
from jax import lax
from jax.experimental import pallas as pl
from jax.experimental.pallas import tpu as pltpu
from jax.sharding import PartitionSpec as P

HD = 128
BLK = 128
NEG_FILL = -1e30
MESH = pl.DeviceIdType.MESH
NT = (((1,), (1,)), ((), ()))


def dot_nn(a, b):
    return jnp.dot(a, b, preferred_element_type=jnp.float32)


def dot_nt(a, b):
    return lax.dot_general(a, b, NT, preferred_element_type=jnp.float32)


def kernel(
    n, nx, nf, topk, mb_dev,
    ids_s, ids_v, x_hbm, w_hbm, lkv_hbm, mkv_hbm, go_hbm,
    att_ref, gin_ref,
    wf, xf, kv, lkv, go, outbox, inbox, ids_in, ids_sm, q32, qb, gq,
    p_send, p_own, s_recv, y_send, y_recv,
    l_sem, i_send, i_recv, i_loc, w_up, w_down, w_x, w_recv, wx_recv,
    x_ysend, x_ssend, x_recv, m_send, m_recv, r_ssend, r_srecv, r_ysend, r_yrecv,
):
    me = lax.axis_index("mem")
    mf = lax.axis_index("fsdp")
    nz = n // nx
    z, xx = me // nx, lax.rem(me, nx)
    ny = nf // 2
    yy, cc = mf // 2, lax.rem(mf, 2)
    sib = mf + 1 - 2 * cc
    dk = wf.shape[1]
    width = wf.shape[2]
    heads = width // HD
    tiles = ids_s.shape[0]
    rows_dev = xf.shape[0] // nf
    ctx = xf.shape[0]

    def local_copy(src, dst, k):
        return pltpu.make_async_copy(src, dst, l_sem.at[k])

    own_x = pl.ds(pl.multiple_of(mf * rows_dev, rows_dev), rows_dev)
    c_w = local_copy(w_hbm, wf.at[me], 0)
    c_x = local_copy(x_hbm, xf.at[own_x, :], 1)
    c_kv = local_copy(mkv_hbm, kv, 2)
    c_lkv = local_copy(lkv_hbm, lkv, 3)
    c_go = local_copy(go_hbm, go, 4)
    c_w.start()
    c_x.start()
    c_kv.start()
    c_lkv.start()
    c_go.start()

    barrier = pltpu.get_barrier_semaphore()

    @pl.loop(1, n)
    def _(d):
        pl.semaphore_signal(
            barrier, inc=1, device_id=(lax.rem(me + d, n), mf), device_id_type=MESH
        )

    pl.semaphore_signal(barrier, inc=1, device_id=(me, sib), device_id_type=MESH)
    for d in range(1, ny):
        pl.semaphore_signal(
            barrier, inc=1, device_id=(me, lax.rem(mf + 2 * d, nf)), device_id_type=MESH
        )
    pl.semaphore_wait(barrier, n - 1 + 1 + ny - 1)

    def remote(src, dst, s, r, dm, df):
        return pltpu.make_async_remote_copy(
            src_ref=src, dst_ref=dst, send_sem=s, recv_sem=r,
            device_id=(dm, df), device_id_type=MESH,
        )

    def id_copy(peer, slot):
        return remote(ids_v, inbox.at[slot], i_send.at[peer], i_recv.at[slot], peer, mf)

    @pl.loop(1, n)
    def _(d):
        id_copy(lax.rem(me + d, n), me).start()

    def w_copy(slot, sem, dst_m, rsem):
        return remote(wf.at[slot], wf.at[slot], sem, rsem, dst_m, mf)

    def w_up_copy(zz):
        return w_copy(zz * nx + xx, w_up.at[zz], me + nx, w_recv.at[zz])

    def w_down_copy(zz):
        return w_copy(zz * nx + xx, w_down.at[zz], me - nx, w_recv.at[zz])

    x_next = z * nx + lax.rem(xx + 1, nx)

    def w_x_copy(r, zz):
        slot = zz * nx + lax.rem(xx - r + nx, nx)
        return w_copy(slot, w_x.at[r, zz], x_next, wx_recv.at[r, zz])

    def w_x_arrival(r, zz):
        slot = zz * nx + lax.rem(xx - 1 - r + 2 * nx, nx)
        return w_copy(slot, w_x.at[r, zz], x_next, wx_recv.at[r, zz])

    c_w.wait()

    @pl.when(z + 1 < nz)
    def _():
        w_up_copy(z).start()

    @pl.when(z > 0)
    def _():
        w_down_copy(z).start()

    w_x_copy(0, z).start()
    c_x.wait()

    def x_rows(f):
        return xf.at[pl.ds(pl.multiple_of(f * rows_dev, rows_dev), rows_dev), :]

    def x_ycopy(d):
        return remote(
            x_rows(mf), x_rows(mf), x_ysend.at[d], x_recv.at[mf], me, lax.rem(mf + 2 * d, nf)
        )

    def x_scopy(f):
        return remote(x_rows(f), x_rows(f), x_ssend.at[f], x_recv.at[f], me, sib)

    for d in range(1, ny):
        x_ycopy(d).start()
    x_scopy(mf).start()

    for k in range(1, nz):
        @pl.when(z - k >= 0)
        def _():
            w_up_copy(z - k).wait_recv()

            @pl.when(z + 1 < nz)
            def _():
                w_up_copy(z - k).start()

            w_x_copy(0, z - k).start()

        @pl.when(z + k < nz)
        def _():
            w_down_copy(z + k).wait_recv()

            @pl.when(z > 0)
            def _():
                w_down_copy(z + k).start()

            w_x_copy(0, z + k).start()

        if k == 1:
            @pl.loop(1, n)
            def _(d):
                src = lax.rem(me + d, n)
                id_copy(src, src).wait_recv()

            c_ids = pltpu.make_async_copy(inbox, ids_sm, i_loc.at[0])
            c_ids.start()
            c_kv.wait()
            c_ids.wait()

            @pl.loop(1, n)
            def _(d):
                peer = lax.rem(me + d, n)
                want = jnp.int32(0)
                for j in range(tiles * topk):
                    one = ids_sm[peer, 0, j]
                    want = jnp.where(one // mb_dev == me, lax.rem(one, mb_dev), want)
                outbox[peer] = kv[want]

            @pl.loop(1, n)
            def _(d):
                peer = lax.rem(me + d, n)
                remote(
                    outbox.at[peer], ids_in.at[me], m_send.at[peer], m_recv.at[me], peer, mf
                ).start()

            mine = jnp.int32(0)
            for j in range(tiles * topk):
                one = ids_s[j // topk, j % topk]
                mine = jnp.where(one // mb_dev == me, lax.rem(one, mb_dev), mine)
            ids_in[me] = kv[mine]

    for d in range(1, ny):
        f = lax.rem(mf + 2 * d, nf)
        x_scopy(f).wait_recv()
        x_scopy(f).start()
    for r in range(nx - 1):
        for zz in range(nz):
            w_x_arrival(r, zz).wait_recv()
            if r + 1 < nx - 1:
                w_x_copy(r + 1, zz).start()
    for d in range(ny):
        x_scopy(lax.rem(sib + 2 * d, nf)).wait_recv()

    q32[...] = jnp.zeros_like(q32)

    @pl.loop(0, n)
    def _(m):
        q32[...] += dot_nn(xf[:, pl.ds(pl.multiple_of(m * dk, dk), dk)], wf[m])

    qb[...] = q32[...].astype(jnp.bfloat16)
    c_lkv.wait()
    c_go.wait()

    @pl.loop(1, n)
    def _(d):
        src = lax.rem(me + d, n)
        remote(
            outbox.at[src], ids_in.at[src], m_send.at[src], m_recv.at[src], src, mf
        ).wait_recv()

    scale = 1.0 / math.sqrt(HD)

    @pl.loop(0, tiles)
    def _(t):
        rows = pl.ds(pl.multiple_of(t * BLK, BLK), BLK)
        owners = [ids_s[t, j] // mb_dev for j in range(topk)]
        causal = lax.broadcasted_iota(jnp.int32, (BLK, ctx), 0) + t * BLK >= (
            lax.broadcasted_iota(jnp.int32, (BLK, ctx), 1)
        )

        @pl.loop(0, heads)
        def _(h):
            cols = pl.ds(pl.multiple_of(h * HD, HD), HD)
            q = qb[rows, cols]
            g = go[rows, cols]
            keys = [ids_in[o, 0, :, cols] for o in owners]
            vals = [ids_in[o, 1, :, cols] for o in owners]
            mk = jnp.concatenate(keys, axis=0)
            mv = jnp.concatenate(vals, axis=0)
            lk = lkv[0, :, cols]
            lv = lkv[1, :, cols]
            s_m = dot_nt(q, mk) * scale
            s_l = jnp.where(causal, dot_nt(q, lk) * scale, NEG_FILL)
            top = jnp.maximum(
                jnp.max(s_m, axis=1, keepdims=True), jnp.max(s_l, axis=1, keepdims=True)
            )
            e_m = jnp.exp(s_m - top)
            e_l = jnp.exp(s_l - top)
            inv = 1.0 / (
                jnp.sum(e_m, axis=1, keepdims=True) + jnp.sum(e_l, axis=1, keepdims=True)
            )
            p_m = e_m * inv
            p_l = e_l * inv
            att_ref[rows, cols] = (
                dot_nn(p_m.astype(jnp.bfloat16), mv) + dot_nn(p_l.astype(jnp.bfloat16), lv)
            ).astype(jnp.bfloat16)
            d_m = dot_nt(g, mv)
            d_l = dot_nt(g, lv)
            delta = jnp.sum(p_m * d_m, axis=1, keepdims=True) + jnp.sum(
                p_l * d_l, axis=1, keepdims=True
            )
            ds_m = (p_m * (d_m - delta)).astype(jnp.bfloat16)
            ds_l = (p_l * (d_l - delta)).astype(jnp.bfloat16)
            gq[rows, cols] = ((dot_nn(ds_m, mk) + dot_nn(ds_l, lk)) * scale).astype(jnp.bfloat16)

    def rs_s(d):
        return remote(p_send.at[d], s_recv.at[d], r_ssend.at[d], r_srecv.at[d], me, sib)

    def rs_y(d):
        return remote(
            y_send.at[d], y_recv.at[d], r_ysend.at[d], r_yrecv.at[d], me,
            lax.rem(mf + 2 * d, nf),
        )

    def share(f, dst, d):
        grad = gq[pl.ds(pl.multiple_of(f * rows_dev, rows_dev), rows_dev), :]

        @pl.loop(0, n)
        def _(m):
            dst[d, m] = dot_nt(grad, wf[m]).astype(jnp.bfloat16)

    order = list(range(1, ny)) + [0]
    for d in order:
        share(lax.rem(sib + 2 * d, nf), p_send, d)
        rs_s(d).start()
    for d in order:
        share(lax.rem(mf + 2 * d, nf), p_own, d)
        rs_s(d).wait_recv()
        if d:
            y_send[d] = (
                p_own[d].astype(jnp.float32) + s_recv[d].astype(jnp.float32)
            ).astype(jnp.bfloat16)
            rs_y(d).start()
    for d in range(1, ny):
        rs_y(d).wait_recv()
    for m in range(n):
        total = p_own[0, m].astype(jnp.float32) + s_recv[0, m].astype(jnp.float32)
        for d in range(1, ny):
            total = total + y_recv[d, m].astype(jnp.float32)
        gin_ref[:, m * dk:(m + 1) * dk] = total.astype(jnp.bfloat16)

    @pl.loop(1, n)
    def _(d):
        peer = lax.rem(me + d, n)
        id_copy(peer, me).wait_send()
        remote(
            outbox.at[peer], ids_in.at[me], m_send.at[peer], m_recv.at[me], peer, mf
        ).wait_send()

    for zz in range(nz):
        @pl.when((zz <= z) & (z + 1 < nz))
        def _():
            w_up_copy(zz).wait_send()

        @pl.when((zz >= z) & (z > 0))
        def _():
            w_down_copy(zz).wait_send()

        for r in range(nx - 1):
            w_x_copy(r, zz).wait_send()
    for d in range(ny):
        if d:
            x_ycopy(d).wait_send()
            rs_y(d).wait_send()
        x_scopy(lax.rem(mf + 2 * d, nf)).wait_send()
        rs_s(d).wait_send()


def local(n, nf, layer_input, w_query, local_kv, memory_kv, memory_ids, grad_out):
    nx = 2 ** ((n.bit_length() - 1) // 2)
    nz = n // nx
    ny = nf // 2
    rows_dev, d_model = layer_input.shape
    dk, width = w_query.shape
    ctx = rows_dev * nf
    tiles, topk = memory_ids.shape
    mb_dev = memory_kv.shape[0]
    flat = memory_ids.reshape(1, tiles * topk)
    ids_v = jnp.pad(flat, ((0, 7), (0, 128 - tiles * topk)))
    bf, f32, i32 = jnp.bfloat16, jnp.float32, jnp.int32
    any_spec = pl.BlockSpec(memory_space=pl.ANY)
    vmem_spec = pl.BlockSpec(memory_space=pltpu.VMEM)
    dma = pltpu.SemaphoreType.DMA
    part = pltpu.VMEM((ny, n, rows_dev, dk), bf)
    return pl.pallas_call(
        functools.partial(kernel, n, nx, nf, topk, mb_dev),
        out_shape=(
            jax.ShapeDtypeStruct((ctx, width), bf),
            jax.ShapeDtypeStruct((rows_dev, d_model), bf),
        ),
        in_specs=[pl.BlockSpec(memory_space=pltpu.SMEM), vmem_spec] + [any_spec] * 5,
        out_specs=(vmem_spec, vmem_spec),
        scratch_shapes=[
            pltpu.VMEM((n, dk, width), bf),
            pltpu.VMEM((ctx, d_model), bf),
            pltpu.VMEM(memory_kv.shape, bf),
            pltpu.VMEM(local_kv.shape, bf),
            pltpu.VMEM(grad_out.shape, bf),
            pltpu.VMEM((n,) + memory_kv.shape[1:], bf),
            pltpu.VMEM((n, 8, 128), i32),
            pltpu.VMEM((n,) + memory_kv.shape[1:], bf),
            pltpu.SMEM((n, 8, 128), i32),
            pltpu.VMEM((ctx, width), f32),
            pltpu.VMEM((ctx, width), bf),
            pltpu.VMEM((ctx, width), bf),
            part, part, part, part, part,
            dma((5,)), dma((n,)), dma((n,)), dma((1,)),
            dma((nz,)), dma((nz,)), dma((max(nx - 1, 1), nz)), dma((nz,)),
            dma((max(nx - 1, 1), nz)),
            dma((ny,)), dma((nf,)), dma((nf,)), dma((n,)), dma((n,)),
            dma((ny,)), dma((ny,)), dma((ny,)), dma((ny,)),
        ],
        compiler_params=pltpu.CompilerParams(
            collective_id=0, has_side_effects=True, vmem_limit_bytes=62 * 1024 * 1024
        ),
    )(memory_ids, ids_v, layer_input, w_query, local_kv, memory_kv, grad_out)


def solution(mesh):
    placed = (
        P(("mem", "fsdp"), None),
        P("mem", "fsdp"),
        P(None, "mem", "fsdp"),
        P("mem", None, None, "fsdp"),
        P("mem", None),
        P("mem", "fsdp"),
    )
    return jax.shard_map(
        functools.partial(local, mesh.shape["mem"], mesh.shape["fsdp"]),
        mesh=mesh,
        in_specs=placed,
        out_specs=(P("mem", "fsdp"), P(("mem", "fsdp"), None)),
        check_vma=False,
    )
```

time: 232 us -> 149 us (0.64)
  Pallas kernels: 0 us -> 142 us
  waiting for transfers between devices: 123 us -> 0 us
  matrix products: 40.6 us -> 0 us
  local copies, waits for them, and re-layouts: 23.8 us -> 5.52 us
  blocking collectives: 13.6 us -> 0 us
  between operations: 14 us -> 0.64 us
  other arithmetic: 12.8 us -> 0 us
  starting transfers between devices: 3.72 us -> 0 us
    pallas_call x0 -> x1, Pallas kernels: none -> 142 us  [local(): pl.pallas_call(functools.partial(kernel, n, nx, nf, topk, mb_dev), out_sh...]
    all_to_all x1 -> x0, waiting for transfers between devices: 60.2 us -> none  [local(): lax.all_to_all(outgoing, 'mem', split_axis=0, concat_axis=0, tiled=True)]
    dot_general x10 -> x0, matrix products: 40.6 us -> none  [the longest x1 6.63 us: local(): jnp.dot(lax.all_gather(layer_input, 'fsdp', axis=0, tiled=True), weight_s...]
    reduce_scatter x1 -> x0, waiting for transfers between devices: 34.2 us -> none  [local(): lax.psum_scatter(lax.dot_general(grad_queries, weight_slice, (((1,), (1,)...]
    all_gather x2 -> x0, waiting for transfers between devices: 26.8 us -> none  [the longest x1 26.8 us: local(): weight_slice = lax.all_gather(w_query, 'mem', axis=0, tiled=True)]
    all_to_all x1 -> x0, blocking collectives: 13.6 us -> none  [local(): lax.all_to_all(wanted_local, 'mem', split_axis=0, concat_axis=0, tiled=True)]
    another operation x4 -> x0, local copies, waits for them, and re-layouts: 9.45 us -> none  [the longest x1 3.99 us: attend_context(): tile_kv[:, :, 1].reshape(tiles_count, mem_keys_count, heads_count, HD)]
    gather x2 -> x0, local copies, waits for them, and re-layouts: 5.66 us -> none  [the longest x1 2.87 us: local(): outgoing = jnp.take(memory_kv, asked[:, 0], axis=0)]
  transfers between devices with their start and end apart: 4 -> 0, of which waited for: 3 -> 0; matrix products, arithmetic and copies ran while one was open for 14% -> 0% of each run, Pallas kernels for 0% -> 0%
where the time goes in v1:
time: 149 us; the launch traced here: 148 us
  Pallas kernels  142 us (95%)
  local copies, waits for them, and re-layouts  5.52 us (4%)
    pallas_call x1, Pallas kernels, local(): pl.pallas_call(functools.partial(kernel, n, nx, nf, topk, mb_dev), out_sh...  142 us
    unnamed x2, local copies, waits for them, and re-layouts  4.16 us

profile of v1, /device:TPU:0, one launch (start us, length us, event | category | flops | bytes accessed | tf_op | source)
XLA Modules:
  0.0 148.3 jit_solution(4410518517167804166)
XLA Ops:
  0.6 0.8 reshape.7
  1.4 0.6 pad.4.ids_v
  2.0 142.1 %shard_map.77 = (bf16[512,512]{1,0:T(8,128)(2,1)}, bf16[128,4096]{1,0:T(8,128)(2,1)}) custom-call(s32[4,4]{1,0:T(4,128)} %ids_s.1, s32[8,128]{1,0:T(8,128)} %pad.4.ids_v, bf16[128,4096]{1,0:T(8,128)(2,1)} %x_hbm.1, bf16[512,512]{1,0:T(8,128)(2,1)} %w_hbm.1, bf16[2,512,512]{2,1,0:T(8,128)(2,1)} %lkv_hbm.1, bf16[16,2,128,512]{3,2,1,0:T(8,128)(2,1)} %mkv_hbm.1, ...), custom_call_target="tpu_custom_call" | custom-call | tf_op jit(solution)/shard_map/pallas_call | solution.py:346
  144.1 1.9 %copy.10 = bf16[512,512]{1,0:T(8,128)(2,1)} copy(bf16[512,512]{1,0:T(8,128)(2,1)} %get-tuple-element.4) | data formatting | bytes 1048576
  146.0 2.3 %copy.11 = bf16[128,4096]{1,0:T(8,128)(2,1)} copy(bf16[128,4096]{1,0:T(8,128)(2,1)} %get-tuple-element.5) | data formatting | bytes 2097152

commit v2 on v1

--- a/solution.py
+++ b/solution.py
@@ -24,11 +24,11 @@
 
 
 def kernel(
-    n, nx, nf, topk, mb_dev,
+    n, nx, nf, topk, mb_dev, pre, parts,
     ids_s, ids_v, x_hbm, w_hbm, lkv_hbm, mkv_hbm, go_hbm,
     att_ref, gin_ref,
     wf, xf, kv, lkv, go, outbox, inbox, ids_in, ids_sm, q32, qb, gq,
-    p_send, p_own, s_recv, y_send, y_recv,
+    p_send, p_own, s_recv, y_send, y_recv, s_mem, d_mem, s_loc, d_loc,
     l_sem, i_send, i_recv, i_loc, w_up, w_down, w_x, w_recv, wx_recv,
     x_ysend, x_ssend, x_recv, m_send, m_recv, r_ssend, r_srecv, r_ysend, r_yrecv,
 ):
@@ -136,6 +136,49 @@
         x_ycopy(d).start()
     x_scopy(mf).start()
 
+    @pl.loop(1, n)
+    def _(d):
+        src = lax.rem(me + d, n)
+        id_copy(src, src).wait_recv()
+
+    c_ids = pltpu.make_async_copy(inbox, ids_sm, i_loc.at[0])
+    c_ids.start()
+    c_kv.wait()
+    c_ids.wait()
+
+    @pl.loop(1, n)
+    def _(d):
+        peer = lax.rem(me + d, n)
+        want = jnp.int32(0)
+        for j in range(tiles * topk):
+            one = ids_sm[peer, 0, j]
+            want = jnp.where(one // mb_dev == me, lax.rem(one, mb_dev), want)
+        outbox[peer] = kv[want]
+
+    mine = jnp.int32(0)
+    for j in range(tiles * topk):
+        one = ids_s[j // topk, j % topk]
+        mine = jnp.where(one // mb_dev == me, lax.rem(one, mb_dev), mine)
+    ids_in[me] = kv[mine]
+
+    def block_copy(peer, slot):
+        return remote(
+            outbox.at[peer], ids_in.at[slot], m_send.at[peer], m_recv.at[slot], peer, mf
+        )
+
+    def send_blocks(k):
+        @pl.loop(1, n)
+        def _(d):
+            peer = lax.rem(me + d, n)
+            pz = peer // nx
+            up = (pz > z) & (jnp.maximum(z, 1) == k)
+            down = (pz < z) & (jnp.maximum(nz - 1 - z, 1) == k)
+            level = (pz == z) & (k == nz - 1)
+
+            @pl.when(up | down | level)
+            def _():
+                block_copy(peer, me).start()
+
     for k in range(1, nz):
         @pl.when(z - k >= 0)
         def _():
@@ -157,38 +200,7 @@
 
             w_x_copy(0, z + k).start()
 
-        if k == 1:
-            @pl.loop(1, n)
-            def _(d):
-                src = lax.rem(me + d, n)
-                id_copy(src, src).wait_recv()
-
-            c_ids = pltpu.make_async_copy(inbox, ids_sm, i_loc.at[0])
-            c_ids.start()
-            c_kv.wait()
-            c_ids.wait()
-
-            @pl.loop(1, n)
-            def _(d):
-                peer = lax.rem(me + d, n)
-                want = jnp.int32(0)
-                for j in range(tiles * topk):
-                    one = ids_sm[peer, 0, j]
-                    want = jnp.where(one // mb_dev == me, lax.rem(one, mb_dev), want)
-                outbox[peer] = kv[want]
-
-            @pl.loop(1, n)
-            def _(d):
-                peer = lax.rem(me + d, n)
-                remote(
-                    outbox.at[peer], ids_in.at[me], m_send.at[peer], m_recv.at[me], peer, mf
-                ).start()
-
-            mine = jnp.int32(0)
-            for j in range(tiles * topk):
-                one = ids_s[j // topk, j % topk]
-                mine = jnp.where(one // mb_dev == me, lax.rem(one, mb_dev), mine)
-            ids_in[me] = kv[mine]
+        send_blocks(k)
 
     for d in range(1, ny):
         f = lax.rem(mf + 2 * d, nf)
@@ -212,36 +224,63 @@
     c_lkv.wait()
     c_go.wait()
 
+    scale = 1.0 / math.sqrt(HD)
+
+    def head_cols(h):
+        return pl.ds(pl.multiple_of(h * HD, HD), HD)
+
+    def block_scores(o):
+        @pl.loop(0, heads)
+        def _(h):
+            cols = head_cols(h)
+            s_mem[h, o] = dot_nt(qb[:, cols], ids_in[o, 0, :, cols]) * scale
+            d_mem[h, o] = dot_nt(go[:, cols], ids_in[o, 1, :, cols])
+
+    if pre:
+        @pl.loop(0, heads)
+        def _(h):
+            cols = head_cols(h)
+            causal = lax.broadcasted_iota(jnp.int32, (ctx, ctx), 0) >= (
+                lax.broadcasted_iota(jnp.int32, (ctx, ctx), 1)
+            )
+            s_loc[h] = jnp.where(causal, dot_nt(qb[:, cols], lkv[0, :, cols]) * scale, NEG_FILL)
+            d_loc[h] = dot_nt(go[:, cols], lkv[1, :, cols])
+
+        block_scores(me)
+
     @pl.loop(1, n)
     def _(d):
         src = lax.rem(me + d, n)
-        remote(
-            outbox.at[src], ids_in.at[src], m_send.at[src], m_recv.at[src], src, mf
-        ).wait_recv()
-
-    scale = 1.0 / math.sqrt(HD)
-
-    @pl.loop(0, tiles)
-    def _(t):
+        block_copy(src, src).wait_recv()
+        if pre:
+            block_scores(src)
+
+    def attend(t):
         rows = pl.ds(pl.multiple_of(t * BLK, BLK), BLK)
         owners = [ids_s[t, j] // mb_dev for j in range(topk)]
-        causal = lax.broadcasted_iota(jnp.int32, (BLK, ctx), 0) + t * BLK >= (
-            lax.broadcasted_iota(jnp.int32, (BLK, ctx), 1)
-        )
 
         @pl.loop(0, heads)
         def _(h):
-            cols = pl.ds(pl.multiple_of(h * HD, HD), HD)
-            q = qb[rows, cols]
-            g = go[rows, cols]
-            keys = [ids_in[o, 0, :, cols] for o in owners]
-            vals = [ids_in[o, 1, :, cols] for o in owners]
-            mk = jnp.concatenate(keys, axis=0)
-            mv = jnp.concatenate(vals, axis=0)
+            cols = head_cols(h)
+            mk = jnp.concatenate([ids_in[o, 0, :, cols] for o in owners], axis=0)
+            mv = jnp.concatenate([ids_in[o, 1, :, cols] for o in owners], axis=0)
             lk = lkv[0, :, cols]
             lv = lkv[1, :, cols]
-            s_m = dot_nt(q, mk) * scale
-            s_l = jnp.where(causal, dot_nt(q, lk) * scale, NEG_FILL)
+            if pre:
+                s_m = jnp.concatenate([s_mem[h, o, rows, :] for o in owners], axis=1)
+                d_m = jnp.concatenate([d_mem[h, o, rows, :] for o in owners], axis=1)
+                s_l = s_loc[h, rows, :]
+                d_l = d_loc[h, rows, :]
+            else:
+                q = qb[rows, cols]
+                g = go[rows, cols]
+                causal = lax.broadcasted_iota(jnp.int32, (BLK, ctx), 0) + t * BLK >= (
+                    lax.broadcasted_iota(jnp.int32, (BLK, ctx), 1)
+                )
+                s_m = dot_nt(q, mk) * scale
+                s_l = jnp.where(causal, dot_nt(q, lk) * scale, NEG_FILL)
+                d_m = dot_nt(g, mv)
+                d_l = dot_nt(g, lv)
             top = jnp.maximum(
                 jnp.max(s_m, axis=1, keepdims=True), jnp.max(s_l, axis=1, keepdims=True)
             )
@@ -255,8 +294,6 @@
             att_ref[rows, cols] = (
                 dot_nn(p_m.astype(jnp.bfloat16), mv) + dot_nn(p_l.astype(jnp.bfloat16), lv)
             ).astype(jnp.bfloat16)
-            d_m = dot_nt(g, mv)
-            d_l = dot_nt(g, lv)
             delta = jnp.sum(p_m * d_m, axis=1, keepdims=True) + jnp.sum(
                 p_l * d_l, axis=1, keepdims=True
             )
@@ -264,36 +301,59 @@
             ds_l = (p_l * (d_l - delta)).astype(jnp.bfloat16)
             gq[rows, cols] = ((dot_nn(ds_m, mk) + dot_nn(ds_l, lk)) * scale).astype(jnp.bfloat16)
 
-    def rs_s(d):
-        return remote(p_send.at[d], s_recv.at[d], r_ssend.at[d], r_srecv.at[d], me, sib)
-
-    def rs_y(d):
+    per = n // parts
+
+    def shards(p):
+        return pl.ds(p * per, per)
+
+    def rs_s(d, p):
         return remote(
-            y_send.at[d], y_recv.at[d], r_ysend.at[d], r_yrecv.at[d], me,
-            lax.rem(mf + 2 * d, nf),
-        )
-
-    def share(f, dst, d):
+            p_send.at[d, shards(p)], s_recv.at[d, shards(p)],
+            r_ssend.at[d, p], r_srecv.at[d, p], me, sib,
+        )
+
+    def rs_y(d, p):
+        return remote(
+            y_send.at[d, shards(p)], y_recv.at[d, shards(p)],
+            r_ysend.at[d, p], r_yrecv.at[d, p], me, lax.rem(mf + 2 * d, nf),
+        )
+
+    def queries_of(f):
+        for i in range(rows_dev // BLK):
+            attend(f * (rows_dev // BLK) + i)
+
+    def share(f, dst, d, p):
         grad = gq[pl.ds(pl.multiple_of(f * rows_dev, rows_dev), rows_dev), :]
 
-        @pl.loop(0, n)
+        @pl.loop(p * per, (p + 1) * per)
         def _(m):
             dst[d, m] = dot_nt(grad, wf[m]).astype(jnp.bfloat16)
 
-    order = list(range(1, ny)) + [0]
-    for d in order:
-        share(lax.rem(sib + 2 * d, nf), p_send, d)
-        rs_s(d).start()
-    for d in order:
-        share(lax.rem(mf + 2 * d, nf), p_own, d)
-        rs_s(d).wait_recv()
-        if d:
-            y_send[d] = (
-                p_own[d].astype(jnp.float32) + s_recv[d].astype(jnp.float32)
-            ).astype(jnp.bfloat16)
-            rs_y(d).start()
-    for d in range(1, ny):
-        rs_y(d).wait_recv()
+    @pl.loop(0, ny)
+    def _(i):
+        d = lax.rem(i + 1, ny)
+        f_sib = lax.rem(sib + 2 * d, nf)
+        f_own = lax.rem(mf + 2 * d, nf)
+        queries_of(f_sib)
+        for p in range(parts):
+            share(f_sib, p_send, d, p)
+            rs_s(d, p).start()
+        queries_of(f_own)
+        for p in range(parts):
+            share(f_own, p_own, d, p)
+            rs_s(d, p).wait_recv()
+
+            @pl.when(d > 0)
+            def _():
+                for m in range(p * per, (p + 1) * per):
+                    y_send[d, m] = (
+                        p_own[d, m].astype(jnp.float32) + s_recv[d, m].astype(jnp.float32)
+                    ).astype(jnp.bfloat16)
+                rs_y(d, p).start()
+
+    for p in range(parts):
+        for d in range(1, ny):
+            rs_y(d, p).wait_recv()
     for m in range(n):
         total = p_own[0, m].astype(jnp.float32) + s_recv[0, m].astype(jnp.float32)
         for d in range(1, ny):
@@ -304,9 +364,7 @@
     def _(d):
         peer = lax.rem(me + d, n)
         id_copy(peer, me).wait_send()
-        remote(
-            outbox.at[peer], ids_in.at[me], m_send.at[peer], m_recv.at[me], peer, mf
-        ).wait_send()
+        block_copy(peer, me).wait_send()
 
     for zz in range(nz):
         @pl.when((zz <= z) & (z + 1 < nz))
@@ -322,9 +380,11 @@
     for d in range(ny):
         if d:
             x_ycopy(d).wait_send()
-            rs_y(d).wait_send()
         x_scopy(lax.rem(mf + 2 * d, nf)).wait_send()
-        rs_s(d).wait_send()
+        for p in range(parts):
+            rs_s(d, p).wait_send()
+            if d:
+                rs_y(d, p).wait_send()
 
 
 def local(n, nf, layer_input, w_query, local_kv, memory_kv, memory_ids, grad_out):
@@ -342,9 +402,14 @@
     any_spec = pl.BlockSpec(memory_space=pl.ANY)
     vmem_spec = pl.BlockSpec(memory_space=pltpu.VMEM)
     dma = pltpu.SemaphoreType.DMA
+    heads = width // HD
+    pre = 2 * heads * ctx * (n * BLK + ctx) * 4 <= 25 * 1024 * 1024
+    parts = math.gcd(n, 4)
+    mem_grid = pltpu.VMEM((heads, n, ctx, BLK) if pre else (8, 128), f32)
+    loc_grid = pltpu.VMEM((heads, ctx, ctx) if pre else (8, 128), f32)
     part = pltpu.VMEM((ny, n, rows_dev, dk), bf)
     return pl.pallas_call(
-        functools.partial(kernel, n, nx, nf, topk, mb_dev),
+        functools.partial(kernel, n, nx, nf, topk, mb_dev, pre, parts),
         out_shape=(
             jax.ShapeDtypeStruct((ctx, width), bf),
             jax.ShapeDtypeStruct((rows_dev, d_model), bf),
@@ -364,12 +429,12 @@
             pltpu.VMEM((ctx, width), f32),
             pltpu.VMEM((ctx, width), bf),
             pltpu.VMEM((ctx, width), bf),
-            part, part, part, part, part,
+            part, part, part, part, part, mem_grid, mem_grid, loc_grid, loc_grid,
             dma((5,)), dma((n,)), dma((n,)), dma((1,)),
             dma((nz,)), dma((nz,)), dma((max(nx - 1, 1), nz)), dma((nz,)),
             dma((max(nx - 1, 1), nz)),
             dma((ny,)), dma((nf,)), dma((nf,)), dma((n,)), dma((n,)),
-            dma((ny,)), dma((ny,)), dma((ny,)), dma((ny,)),
+            dma((ny, parts)), dma((ny, parts)), dma((ny, parts)), dma((ny, parts)),
         ],
         compiler_params=pltpu.CompilerParams(
             collective_id=0, has_side_effects=True, vmem_limit_bytes=62 * 1024 * 1024

time: 149 us -> 148 us (level)
  no operation moved by 1% of the time
where the time goes in v2:
time: 148 us
  Pallas kernels  142 us (96%)
  local copies, waits for them, and re-layouts  5.52 us (4%)
    pallas_call x1, Pallas kernels, local(): pl.pallas_call(functools.partial(kernel, n, nx, nf, topk, mb_dev, pre, pa...  142 us
    unnamed x2, local copies, waits for them, and re-layouts  4.16 us

profile of v2, /device:TPU:0, one launch (start us, length us, event | category | flops | bytes accessed | tf_op | source)
XLA Modules:
  0.0 147.8 jit_solution(12638476544140150871)
XLA Ops:
  0.6 0.8 reshape.7
  1.4 0.6 pad.4.ids_v
  2.0 141.6 %shard_map.77 = (bf16[512,512]{1,0:T(8,128)(2,1)}, bf16[128,4096]{1,0:T(8,128)(2,1)}) custom-call(s32[4,4]{1,0:T(4,128)} %ids_s.1, s32[8,128]{1,0:T(8,128)} %pad.4.ids_v, bf16[128,4096]{1,0:T(8,128)(2,1)} %x_hbm.1, bf16[512,512]{1,0:T(8,128)(2,1)} %w_hbm.1, bf16[2,512,512]{2,1,0:T(8,128)(2,1)} %lkv_hbm.1, bf16[16,2,128,512]{3,2,1,0:T(8,128)(2,1)} %mkv_hbm.1, ...), custom_call_target="tpu_custom_call" | custom-call | tf_op jit(solution)/shard_map/pallas_call | solution.py:411
  143.6 1.9 %copy.10 = bf16[512,512]{1,0:T(8,128)(2,1)} copy(bf16[512,512]{1,0:T(8,128)(2,1)} %get-tuple-element.4) | data formatting | bytes 1048576
  145.5 2.3 %copy.11 = bf16[128,4096]{1,0:T(8,128)(2,1)} copy(bf16[128,4096]{1,0:T(8,128)(2,1)} %get-tuple-element.5) | data formatting | bytes 2097152

commit v3 on v2

--- a/solution.py
+++ b/solution.py
@@ -170,12 +170,9 @@
         @pl.loop(1, n)
         def _(d):
             peer = lax.rem(me + d, n)
-            pz = peer // nx
-            up = (pz > z) & (jnp.maximum(z, 1) == k)
-            down = (pz < z) & (jnp.maximum(nz - 1 - z, 1) == k)
-            level = (pz == z) & (k == nz - 1)
-
-            @pl.when(up | down | level)
+            column = lax.rem(peer, nx) == xx
+
+            @pl.when((column & (k == 3)) | (jnp.logical_not(column) & (k == 2)))
             def _():
                 block_copy(peer, me).start()
 
@@ -206,19 +203,34 @@
         f = lax.rem(mf + 2 * d, nf)
         x_scopy(f).wait_recv()
         x_scopy(f).start()
+    for d in range(ny):
+        x_scopy(lax.rem(sib + 2 * d, nf)).wait_recv()
+
+    q32[...] = jnp.zeros_like(q32)
+
+    def project(slot):
+        q32[...] += dot_nn(xf[:, pl.ds(pl.multiple_of(slot * dk, dk), dk)], wf[slot])
+
+    def by_distance(body):
+        body(z)
+        for k in range(1, nz):
+            for zz in (z - k, z + k):
+                @pl.when((zz >= 0) & (zz < nz))
+                def _():
+                    body(zz)
+
+    @pl.loop(0, nz)
+    def _(zz):
+        project(zz * nx + xx)
+
     for r in range(nx - 1):
-        for zz in range(nz):
+        def arrived(zz):
             w_x_arrival(r, zz).wait_recv()
             if r + 1 < nx - 1:
                 w_x_copy(r + 1, zz).start()
-    for d in range(ny):
-        x_scopy(lax.rem(sib + 2 * d, nf)).wait_recv()
-
-    q32[...] = jnp.zeros_like(q32)
-
-    @pl.loop(0, n)
-    def _(m):
-        q32[...] += dot_nn(xf[:, pl.ds(pl.multiple_of(m * dk, dk), dk)], wf[m])
+            project(zz * nx + lax.rem(xx - 1 - r + 2 * nx, nx))
+
+        by_distance(arrived)
 
     qb[...] = q32[...].astype(jnp.bfloat16)
     c_lkv.wait()

time: 148 us -> 127 us (0.86)
  Pallas kernels: 142 us -> 120 us
    pallas_call x1, Pallas kernels: 142 us -> 120 us  [local(): pl.pallas_call(functools.partial(kernel, n, nx, nf, topk, mb_dev, pre, pa...]
where the time goes in v3:
time: 127 us
  Pallas kernels  120 us (94%)
  local copies, waits for them, and re-layouts  5.52 us (4%)
    pallas_call x1, Pallas kernels, local(): pl.pallas_call(functools.partial(kernel, n, nx, nf, topk, mb_dev, pre, pa...  120 us
    unnamed x2, local copies, waits for them, and re-layouts  4.16 us

profile of v3, /device:TPU:0, one launch (start us, length us, event | category | flops | bytes accessed | tf_op | source)
XLA Modules:
  0.0 126.5 jit_solution(4351502475721904615)
XLA Ops:
  0.6 0.8 reshape.7
  1.4 0.6 pad.4.ids_v
  2.0 120.4 %shard_map.77 = (bf16[512,512]{1,0:T(8,128)(2,1)}, bf16[128,4096]{1,0:T(8,128)(2,1)}) custom-call(s32[4,4]{1,0:T(4,128)} %ids_s.1, s32[8,128]{1,0:T(8,128)} %pad.4.ids_v, bf16[128,4096]{1,0:T(8,128)(2,1)} %x_hbm.1, bf16[512,512]{1,0:T(8,128)(2,1)} %w_hbm.1, bf16[2,512,512]{2,1,0:T(8,128)(2,1)} %lkv_hbm.1, bf16[16,2,128,512]{3,2,1,0:T(8,128)(2,1)} %mkv_hbm.1, ...), custom_call_target="tpu_custom_call" | custom-call | tf_op jit(solution)/shard_map/pallas_call | solution.py:423
  122.4 1.9 %copy.10 = bf16[512,512]{1,0:T(8,128)(2,1)} copy(bf16[512,512]{1,0:T(8,128)(2,1)} %get-tuple-element.4) | data formatting | bytes 1048576
  124.2 2.3 %copy.11 = bf16[128,4096]{1,0:T(8,128)(2,1)} copy(bf16[128,4096]{1,0:T(8,128)(2,1)} %get-tuple-element.5) | data formatting | bytes 2097152

commit v4 on v3

--- a/solution.py
+++ b/solution.py
@@ -28,7 +28,7 @@
     ids_s, ids_v, x_hbm, w_hbm, lkv_hbm, mkv_hbm, go_hbm,
     att_ref, gin_ref,
     wf, xf, kv, lkv, go, outbox, inbox, ids_in, ids_sm, q32, qb, gq,
-    p_send, p_own, s_recv, y_send, y_recv, s_mem, d_mem, s_loc, d_loc,
+    p_send, p_own, s_recv, y_send, y_recv, s_loc, d_loc,
     l_sem, i_send, i_recv, i_loc, w_up, w_down, w_x, w_recv, wx_recv,
     x_ysend, x_ssend, x_recv, m_send, m_recv, r_ssend, r_srecv, r_ysend, r_yrecv,
 ):
@@ -169,7 +169,7 @@
     def send_blocks(k):
         @pl.loop(1, n)
         def _(d):
-            peer = lax.rem(me + d, n)
+            peer = lax.rem(me + n - d, n)
             column = lax.rem(peer, nx) == xx
 
             @pl.when((column & (k == 3)) | (jnp.logical_not(column) & (k == 2)))
@@ -240,13 +240,6 @@
 
     def head_cols(h):
         return pl.ds(pl.multiple_of(h * HD, HD), HD)
-
-    def block_scores(o):
-        @pl.loop(0, heads)
-        def _(h):
-            cols = head_cols(h)
-            s_mem[h, o] = dot_nt(qb[:, cols], ids_in[o, 0, :, cols]) * scale
-            d_mem[h, o] = dot_nt(go[:, cols], ids_in[o, 1, :, cols])
 
     if pre:
         @pl.loop(0, heads)
@@ -258,14 +251,10 @@
             s_loc[h] = jnp.where(causal, dot_nt(qb[:, cols], lkv[0, :, cols]) * scale, NEG_FILL)
             d_loc[h] = dot_nt(go[:, cols], lkv[1, :, cols])
 
-        block_scores(me)
-
     @pl.loop(1, n)
     def _(d):
         src = lax.rem(me + d, n)
         block_copy(src, src).wait_recv()
-        if pre:
-            block_scores(src)
 
     def attend(t):
         rows = pl.ds(pl.multiple_of(t * BLK, BLK), BLK)
@@ -279,8 +268,8 @@
             lk = lkv[0, :, cols]
             lv = lkv[1, :, cols]
             if pre:
-                s_m = jnp.concatenate([s_mem[h, o, rows, :] for o in owners], axis=1)
-                d_m = jnp.concatenate([d_mem[h, o, rows, :] for o in owners], axis=1)
+                s_m = dot_nt(qb[rows, cols], mk) * scale
+                d_m = dot_nt(go[rows, cols], mv)
                 s_l = s_loc[h, rows, :]
                 d_l = d_loc[h, rows, :]
             else:
@@ -415,9 +404,8 @@
     vmem_spec = pl.BlockSpec(memory_space=pltpu.VMEM)
     dma = pltpu.SemaphoreType.DMA
     heads = width // HD
-    pre = 2 * heads * ctx * (n * BLK + ctx) * 4 <= 25 * 1024 * 1024
+    pre = 2 * heads * ctx * ctx * 4 <= 12 * 1024 * 1024
     parts = math.gcd(n, 4)
-    mem_grid = pltpu.VMEM((heads, n, ctx, BLK) if pre else (8, 128), f32)
     loc_grid = pltpu.VMEM((heads, ctx, ctx) if pre else (8, 128), f32)
     part = pltpu.VMEM((ny, n, rows_dev, dk), bf)
     return pl.pallas_call(
@@ -441,7 +429,7 @@
             pltpu.VMEM((ctx, width), f32),
             pltpu.VMEM((ctx, width), bf),
             pltpu.VMEM((ctx, width), bf),
-            part, part, part, part, part, mem_grid, mem_grid, loc_grid, loc_grid,
+            part, part, part, part, part, loc_grid, loc_grid,
             dma((5,)), dma((n,)), dma((n,)), dma((1,)),
             dma((nz,)), dma((nz,)), dma((max(nx - 1, 1), nz)), dma((nz,)),
             dma((max(nx - 1, 1), nz)),

time: 127 us -> 119 us (0.937)
  Pallas kernels: 120 us -> 113 us
    pallas_call x1, Pallas kernels: 120 us -> 113 us  [local(): pl.pallas_call(functools.partial(kernel, n, nx, nf, topk, mb_dev, pre, pa...]
where the time goes in v4:
time: 119 us
  Pallas kernels  113 us (95%)
  local copies, waits for them, and re-layouts  5.52 us (5%)
    pallas_call x1, Pallas kernels, local(): pl.pallas_call(functools.partial(kernel, n, nx, nf, topk, mb_dev, pre, pa...  113 us
    unnamed x2, local copies, waits for them, and re-layouts  4.16 us

profile of v4, /device:TPU:0, one launch (start us, length us, event | category | flops | bytes accessed | tf_op | source)
XLA Modules:
  0.0 119.2 jit_solution(10023623253128461580)
XLA Ops:
  0.6 0.8 reshape.7
  1.4 0.6 pad.4.ids_v
  2.0 113.1 %shard_map.77 = (bf16[512,512]{1,0:T(8,128)(2,1)}, bf16[128,4096]{1,0:T(8,128)(2,1)}) custom-call(s32[4,4]{1,0:T(4,128)} %ids_s.1, s32[8,128]{1,0:T(8,128)} %pad.4.ids_v, bf16[128,4096]{1,0:T(8,128)(2,1)} %x_hbm.1, bf16[512,512]{1,0:T(8,128)(2,1)} %w_hbm.1, bf16[2,512,512]{2,1,0:T(8,128)(2,1)} %lkv_hbm.1, bf16[16,2,128,512]{3,2,1,0:T(8,128)(2,1)} %mkv_hbm.1, ...), custom_call_target="tpu_custom_call" | custom-call | tf_op jit(solution)/shard_map/pallas_call | solution.py:411
  115.1 1.9 %copy.10 = bf16[512,512]{1,0:T(8,128)(2,1)} copy(bf16[512,512]{1,0:T(8,128)(2,1)} %get-tuple-element.4) | data formatting | bytes 1048576
  116.9 2.3 %copy.11 = bf16[128,4096]{1,0:T(8,128)(2,1)} copy(bf16[128,4096]{1,0:T(8,128)(2,1)} %get-tuple-element.5) | data formatting | bytes 2097152
